TPU v7x, 1024 devices: a whole 4x4x32 slice. The times are simulated.
1024 devices in a mesh: worker: 8 (over y, x_lo), fsdp: 128 (over x_hi, z, core).
Axes of the slice: x: 4 (x_hi: 2, x_lo: 2; x = x_hi * 2 + x_lo), y: 4, z: 32, core: 2. Of those that a mesh axis runs over, the one named last changes fastest.
Arguments:
- params: float32 [8, 4096, 128], P('worker', 'fsdp'), may hold values from -6 to 6
- first_moment: float32 [8, 4096, 128], P('worker', 'fsdp'), may hold values from -4 to 4
- second_moment: float32 [8, 4096, 128], P('worker', 'fsdp'), may hold values from 0.05 to 2
- global_fragment: float32 [1024, 128], P('fsdp'), may hold values from -6 to 6
- outer_momentum: float32 [1024, 128], P('fsdp'), may hold values from -6 to 6
- features: bfloat16 [8, 16384, 4096], P('worker', 'fsdp'), may hold values from -6 to 6
- cotangent: bfloat16 [8, 16384, 128], P('worker', 'fsdp'), may hold values from -768 to 768
- token_counts: int32 [8], replicated, may hold values from 2048 to 16384
- fragment_index: int32 [1], replicated, may hold values from 0 to 3
Outputs:
- new_params: float32 [8, 4096, 128], P('worker', 'fsdp')
- new_first: float32 [8, 4096, 128], P('worker', 'fsdp')
- new_second: float32 [8, 4096, 128], P('worker', 'fsdp')
- new_global: float32 [1024, 128], P('fsdp')
- new_momentum: float32 [1024, 128], P('fsdp')
All inputs are finite; a program needn't handle non-finite values.
Results may differ from a plain program's by a relative error of at most 0.0003.
Values sent between devices are 32-bit elements; how exact they have to be, the bound alone decides.
A program may use at most 32 MiB of HBM per device.

v0:
```python
import jax
import jax.numpy as jnp
from jax import lax
from jax.sharding import PartitionSpec as P

FRAGS = 4


BETA_ONE = 0.9
BETA_TWO = 0.95
CORRECT_ONE = 0.6513216
CORRECT_TWO = 0.401263
ADAM_EPS = 1e-08
LEARN_RATE = 0.02
DECAY_RATE = 0.1
NESTEROV = 0.9
OUTER_RATE = 0.7
MIXING = 0.5


def contract_rows(left_rows, right_rows):
    return lax.dot_general(
        left_rows, right_rows, (((0,), (0,)), ((), ())), preferred_element_type=jnp.float32
    )


def body(
    params,
    first_moment,
    second_moment,
    global_fragment,
    outer_momentum,
    features,
    cotangent,
    token_counts,
    fragment_index,
):
    worker = lax.axis_index("worker")
    live_count = lax.dynamic_index_in_dim(token_counts, worker, 0, keepdims=False)
    tok_local = features.shape[1]
    positions = lax.axis_index("fsdp") * tok_local + lax.iota(jnp.int32, tok_local)
    valid_rows = (positions < live_count)[:, None]
    masked = jnp.where(valid_rows, cotangent[0], jnp.zeros_like(cotangent[0]))
    feats = features[0]
    local_rows = params.shape[1]
    term = contract_rows(feats, masked)
    summed = lax.psum_scatter(term, "fsdp", scatter_dimension=0, tiled=True)
    gradient = summed / live_count.astype(jnp.float32)
    fragment = fragment_index[0]
    width = params.shape[2]
    before = params[0]
    before_three = before.reshape(local_rows // FRAGS, FRAGS, width)
    old_piece = lax.dynamic_index_in_dim(before_three, fragment, 1, keepdims=False)
    token_total = jnp.sum(token_counts).astype(jnp.float32)
    drift_term = live_count.astype(jnp.float32) * (global_fragment - old_piece)
    pseudo_grad = lax.psum(drift_term, "worker") / token_total
    momentum = NESTEROV * outer_momentum + pseudo_grad
    fresh_global = global_fragment - OUTER_RATE * (pseudo_grad + NESTEROV * momentum)
    first_new = BETA_ONE * first_moment[0] + (1.0 - BETA_ONE) * gradient
    second_new = BETA_TWO * second_moment[0] + (1.0 - BETA_TWO) * gradient * gradient
    update = first_new / CORRECT_ONE / (jnp.sqrt(second_new / CORRECT_TWO) + ADAM_EPS)
    inner_params = before - LEARN_RATE * (update + DECAY_RATE * before)
    inner_three = inner_params.reshape(local_rows // FRAGS, FRAGS, width)
    inner_piece = lax.dynamic_index_in_dim(inner_three, fragment, 1, keepdims=False)
    mixed_piece = MIXING * fresh_global + (1.0 - MIXING) * inner_piece
    result = lax.dynamic_update_index_in_dim(inner_three, mixed_piece, fragment, 1).reshape(
        local_rows, width
    )
    return (result[None], first_new[None], second_new[None], fresh_global, momentum)


def solution(mesh):
    placed = (
        P("worker", "fsdp", None),
        P("worker", "fsdp", None),
        P("worker", "fsdp", None),
        P("fsdp", None),
        P("fsdp", None),
        P("worker", "fsdp", None),
        P("worker", "fsdp", None),
        P(),
        P(),
    )
    return jax.shard_map(
        body,
        mesh=mesh,
        in_specs=placed,
        out_specs=(
            P("worker", "fsdp", None),
            P("worker", "fsdp", None),
            P("worker", "fsdp", None),
            P("fsdp", None),
            P("fsdp", None),
        ),
        check_vma=False,
    )
```

profile of v0, /device:TPU:8, one launch (start us, length us, event | category | flops | bytes accessed | tf_op | source)
XLA Modules:
  0.0 439.0 jit_solution(1603939088542952225)
XLA Ops:
  7.2 0.0 copy-start
  7.2 0.0 reduce-scatter.4.cloned.1.call-start
  7.2 1.3 dynamic_slice.11
  8.6 0.7 add_compare_fusion
  9.2 0.0 copy-done
  9.2 1.3 convolution_bitcast_fusion
  10.5 1.8 copy.32
  12.4 0.0 copy-start.7
  12.4 0.0 copy-start.1
  12.4 0.0 copy-start.5
  12.4 0.0 copy-start.3
  12.4 0.0 copy-start.4
  12.4 0.0 copy-start.6
  12.4 0.0 reduce-scatter.4.cloned.1.call-update
  13.1 0.0 copy-done.7
  13.1 0.6 reduce_sum.9
  15.0 0.0 copy-done.1
  15.1 0.0 copy-done.5
  15.1 26.4 %psum.7 = f32[8,128]{1,0:T(8,128)S(1)} all-reduce(f32[8,128]{1,0:T(8,128)S(1)} %subtract_multiply_fusion), channel_id=1, replica_groups=mesh['worker'=8,'fsdp'=128] {'worker'}, use_global_device_ids=true, to_apply=%region_1.2 | all-reduce | flops 1024 | bytes 8192 | tf_op jit(solution)/shard_map/psum | solution.py:56
  41.5 388.0 %reduce-scatter.4.cloned.1.call-done = f32[32,128]{1,0:T(8,128)} async-done(((f32[4096,128]{1,0:T(8,128)}), f32[32,128]{1,0:T(8,128)}) %reduce-scatter.4.cloned.1.call-update) | async-done | bytes 16400 | tf_op jit(solution)/shard_map/reduce_scatter | solution.py:47
  429.5 0.0 copy-done.3
  429.5 0.0 copy-done.4
  429.5 1.3 fusion.10
  430.9 0.0 copy-done.6
  430.9 0.6 add_multiply_fusion
  431.5 0.0 copy-start.2
  431.5 0.6 copy-done.2
  (4 shorter events, 0.1 us)
Async XLA Ops:
  7.2 2.0 copy-start
  7.2 422.3 %reduce-scatter.4.cloned.1.call-start = ((), (), s32[]{:S(2)}) async-start(), calls=%async_computation.1 | async-start | bytes 2113536 | tf_op jit(solution)/shard_map/reduce_scatter | solution.py:47
  12.4 0.7 copy-start.7
  12.4 2.7 copy-start.1
  12.4 2.7 copy-start.5
  12.4 417.1 %copy-start.3 = (f32[1,32,128]{2,1,0:T(8,128)S(1)}, f32[1,32,128]{2,1,0:T(8,128)}, u32[]{:S(2)}) copy-start(f32[1,32,128]{2,1,0:T(8,128)} %param.11) | copy-start | bytes 49156
  12.4 417.1 %copy-start.4 = (f32[1,32,128]{2,1,0:T(8,128)S(1)}, f32[1,32,128]{2,1,0:T(8,128)}, u32[]{:S(2)}) copy-start(f32[1,32,128]{2,1,0:T(8,128)} %param.10) | copy-start | bytes 49156
  12.4 418.5 %copy-start.6 = (f32[8,128]{1,0:T(8,128)S(1)}, f32[8,128]{1,0:T(8,128)}, u32[]{:S(2)}) copy-start(f32[8,128]{1,0:T(8,128)} %param.13) | copy-start | bytes 12292
  431.5 0.6 copy-start.2
Sparse Core Ops, SparseCore 0:
  13.8 415.6 reduce-scatter.3
where the time goes:
time: 439 us
  waiting for transfers between devices  388 us (88%)
  blocking collectives  26.4 us (6%)
  between operations  16.1 us (4%)
    reduce_scatter x1, waiting for transfers between devices, body(): summed = lax.psum_scatter(term, 'fsdp', scatter_dimension=0, tiled=True)  388 us
    psum x1, blocking collectives, body(): pseudo_grad = lax.psum(drift_term, 'worker') / token_total  26.4 us
  transfers between devices with their start and end apart: 1, of which 1 were waited for; matrix products, arithmetic and copies ran while one was open for 0% of the time, Pallas kernels for 0%

commit v1 on v0

v1 whole, which is shorter than its diff:
```python
import functools

import jax
import jax.numpy as jnp
from jax import lax
from jax.experimental import pallas as pl
from jax.experimental.pallas import tpu as pltpu
from jax.sharding import PartitionSpec as P

MESH = pl.DeviceIdType.MESH
F32 = jnp.float32

FRAGS = 4
BETA_ONE = 0.9
BETA_TWO = 0.95
CORRECT_ONE = 0.6513216
CORRECT_TWO = 0.401263
ADAM_EPS = 1e-08
LEARN_RATE = 0.02
DECAY_RATE = 0.1
NESTEROV = 0.9
OUTER_RATE = 0.7
MIXING = 0.5

STRIDE = 3
GROUP = 4


def make_tree(zs, stride):
    steps = {}
    for d, length in ((1, zs // 2), (-1, zs - zs // 2 - 1)):
        stops = list(range(length, stride - 1, -stride))
        if not stops:
            stops = [length]
        for o in range(length, 0, -1):
            if o in stops:
                below = [s for s in stops if s < o]
                steps[d, o] = o - (max(below) if below else 0)
            else:
                steps[d, o] = 1
    return steps


def make_order(steps):
    kids = {}
    for (d, o), s in steps.items():
        up = (d, o - s) if o - s else (0, 0)
        kids.setdefault(up, []).append((d, o))
    half = max(o for _, o in steps)
    ready = {}

    def when(node):
        if node not in ready:
            own = 0.3 * (half - node[1])
            ready[node] = max([own] + [when(k) + 1.0 + 0.8 * steps[k] for k in kids.get(node, [])])
        return ready[node]

    order = sorted(steps, key=lambda n: (when(n), -n[1], -n[0]))
    return order, kids


def kernel(
    nw,
    zs,
    counts,
    frag_ref,
    params_h,
    first_h,
    second_h,
    glob_h,
    mom_h,
    feats_h,
    cot_h,
    new_params,
    new_first,
    new_second,
    new_glob,
    new_mom,
    feats,
    cot,
    params,
    first,
    second,
    glob,
    mom,
    term,
    crecv,
    chip,
    xrecv,
    own,
    zsend,
    zrecv,
    drift,
    wall,
    spread,
    load_sem,
    csend_sem,
    crecv_sem,
    xsend_sem,
    xrecv_sem,
    zsend_sem,
    zrecv_sem,
    wsend_sem,
    wrecv_sem,
):
    w = lax.axis_index("worker")
    k = lax.axis_index("fsdp")
    xh = k // (2 * zs)
    z = (k // 2) % zs
    c = k % 2
    rows = params.shape[0]
    tokens = feats.shape[0]
    groups = zs // GROUP

    steps = make_tree(zs, STRIDE)
    order, kids = make_order(steps)
    slot = {node: i for i, node in enumerate(steps)}
    lengths = sorted({(d, s) for (d, _), s in steps.items()})

    def at(x, zz, core):
        return (w, x * (2 * zs) + zz * 2 + core)

    core_mate = at(xh, z, 1 - c)
    x_mate = at(1 - xh, z, c)

    def z_mate(hop):
        return at(xh, (z + hop + zs) % zs, c)

    partners = [core_mate, x_mate]
    hops = sorted({h for d, s in lengths for h in (d * s, -d * s)})
    partners += [z_mate(h) for h in hops]
    partners += [((w + r) % nw, k) for r in range(1, nw)]
    barrier = pltpu.get_barrier_semaphore()
    for mate in partners:
        pl.semaphore_signal(barrier, inc=1, device_id=mate, device_id_type=MESH)

    loads = []
    for i, (src, dst) in enumerate(
        (
            (cot_h, cot),
            (feats_h, feats),
            (params_h, params),
            (glob_h, glob),
            (first_h, first),
            (second_h, second),
            (mom_h, mom),
        )
    ):
        copy = pltpu.make_async_copy(src, dst, load_sem.at[i])
        copy.start()
        loads.append(copy)

    live = counts[w]
    live_f = live.astype(F32)
    loads[0].wait()
    position = k * tokens + lax.broadcasted_iota(jnp.int32, cot.shape, 0)
    masked = jnp.where(position < live, cot[...], jnp.zeros_like(cot[...]))
    loads[1].wait()

    def group_z(i):
        p = ((i + 1) // 2) * (1 if i % 2 else -1)
        return ((z // GROUP + groups // 2 + p + groups) % groups) * GROUP

    order_of_groups = [((i + 1) // 2) * (1 if i % 2 else -1) % groups for i in range(groups)]

    def remote(src, dst, send, recv, mate):
        return pltpu.make_async_remote_copy(
            src_ref=src, dst_ref=dst, send_sem=send, recv_sem=recv, device_id=mate, device_id_type=MESH
        )

    core_copies, x_copies = [], []

    def multiply(i):
        base = group_z(i)
        for x in range(2):
            for pair in range(GROUP // 2):
                col = pl.multiple_of((x * zs + base + 2 * pair) * (2 * rows), 4 * rows)
                block = lax.dot_general(
                    feats[:, pl.ds(col, 4 * rows)],
                    masked,
                    (((0,), (0,)), ((), ())),
                    preferred_element_type=F32,
                )
                for dz in range(2):
                    for core in range(2):
                        lo = (2 * dz + core) * rows
                        term[core, x, base + 2 * pair + dz] = block[lo : lo + rows]

    def send_core(i):
        zr = pl.ds(group_z(i), GROUP)
        copy = remote(term.at[1 - c, :, zr], crecv.at[:, zr], csend_sem.at[i], crecv_sem.at[i], core_mate)
        copy.start()
        core_copies.append(copy)

    def send_x(i):
        zr = pl.ds(group_z(i), GROUP)
        core_copies[i].wait_recv()
        chip[:, zr] = term[c, :, zr] + crecv[:, zr]
        copy = remote(chip.at[1 - xh, zr], xrecv.at[zr], xsend_sem.at[i], xrecv_sem.at[i], x_mate)
        copy.start()
        x_copies.append(copy)

    multiply(0)
    pl.semaphore_wait(barrier, len(partners))
    send_core(0)
    lag = 3
    for i in range(1, groups):
        multiply(i)
        send_core(i)
        if i >= lag:
            send_x(i - lag)
    for i in range(max(groups - lag, 0), groups):
        send_x(i)

    loads[2].wait()
    loads[3].wait()
    frag = frag_ref[0]
    old = params[pl.ds(0, rows // FRAGS, stride=FRAGS), :]
    for f in range(1, FRAGS):
        old = jnp.where(frag == f, params[pl.ds(f, rows // FRAGS, stride=FRAGS), :], old)
    mine = live_f * (glob[...] - old)
    drift[...] = mine
    wall[w] = mine
    worker_copies = []
    for r in range(1, nw):
        copy = remote(drift, wall.at[w], wsend_sem.at[r], wrecv_sem.at[w], ((w + r) % nw, k))
        copy.start()
        worker_copies.append(copy)

    def outer():
        for r in range(1, nw):
            sender = (w + r) % nw
            remote(drift, wall.at[sender], wsend_sem.at[r], wrecv_sem.at[sender], (sender, k)).wait_recv()
        total = wall[0]
        token_total = counts[0]
        for i in range(1, nw):
            total = total + wall[i]
            token_total = token_total + counts[i]
        pseudo = total / token_total.astype(F32)
        loads[6].wait()
        momentum = NESTEROV * mom[...] + pseudo
        fresh = glob[...] - OUTER_RATE * (pseudo + NESTEROV * momentum)
        new_mom[...] = momentum
        new_glob[...] = fresh
        for f in range(FRAGS):
            spread[pl.ds(f, rows // FRAGS, stride=FRAGS), :] = fresh
        loads[4].wait()
        loads[5].wait()

    done = set()

    def need(d, o):
        rel = {((r + d * o) // GROUP) % groups for r in range(GROUP)}
        for i in range(groups):
            where = (groups // 2 + order_of_groups[i]) % groups
            if where in rel and i not in done:
                done.add(i)
                x_copies[i].wait_recv()
                zr = pl.ds(group_z(i), GROUP)
                own[zr] = chip[xh, zr] + xrecv[zr]

    z_copies = {}

    def gather(node, zz):
        total = own[zz]
        for kid in kids.get(node, []):
            z_copies[kid].wait_recv()
            total = total + zrecv[slot[kid]]
        return total

    for count, node in enumerate(order):
        d, o = node
        need(d, o)
        zz = (z + d * o + zs) % zs
        i = slot[node]
        if kids.get(node):
            zsend[i] = gather(node, zz)
            src = zsend.at[i]
        else:
            src = own.at[zz]
        copy = remote(src, zrecv.at[i], zsend_sem.at[i], zrecv_sem.at[i], z_mate(d * steps[node]))
        copy.start()
        z_copies[node] = copy
        if count == (3 * len(order)) // 4:
            outer()

    need(1, 0)
    gradient = gather((0, 0), z) / live_f
    first_new = BETA_ONE * first[...] + (1.0 - BETA_ONE) * gradient
    second_new = BETA_TWO * second[...] + (1.0 - BETA_TWO) * gradient * gradient
    update = first_new / CORRECT_ONE / (jnp.sqrt(second_new / CORRECT_TWO) + ADAM_EPS)
    before = params[...]
    inner = before - LEARN_RATE * (update + DECAY_RATE * before)
    chosen = lax.broadcasted_iota(jnp.int32, inner.shape, 0) % FRAGS == frag
    new_params[...] = jnp.where(chosen, MIXING * spread[...] + (1.0 - MIXING) * inner, inner)
    new_first[...] = first_new
    new_second[...] = second_new

    for copy in core_copies + x_copies + worker_copies + list(z_copies.values()):
        copy.wait_send()


def solution(mesh):
    nw = mesh.shape["worker"]
    zs = mesh.shape["fsdp"] // 4

    def step(params, first, second, glob, mom, features, cotangent, counts, frag):
        rows, width = params.shape[1:]
        frows = glob.shape[0]
        tokens, depth = features.shape[1:]
        vm = pltpu.VMEM
        dma = pltpu.SemaphoreType.DMA
        messages = zs - 1
        groups = zs // GROUP
        tile = (rows, width)
        big = jax.ShapeDtypeStruct(tile, F32)
        small = jax.ShapeDtypeStruct((frows, width), F32)
        smem = pl.BlockSpec(memory_space=pltpu.SMEM)
        hbm = pl.BlockSpec(memory_space=pl.ANY)
        out = pl.pallas_call(
            functools.partial(kernel, nw, zs),
            out_shape=(big, big, big, small, small),
            in_specs=[smem, smem] + [hbm] * 7,
            out_specs=[pl.BlockSpec(memory_space=vm)] * 5,
            scratch_shapes=[
                vm((tokens, depth), jnp.bfloat16),
                vm((tokens, width), jnp.bfloat16),
                vm(tile, F32),
                vm(tile, F32),
                vm(tile, F32),
                vm((frows, width), F32),
                vm((frows, width), F32),
                vm((2, 2, zs) + tile, F32),
                vm((2, zs) + tile, F32),
                vm((2, zs) + tile, F32),
                vm((zs,) + tile, F32),
                vm((zs,) + tile, F32),
                vm((messages,) + tile, F32),
                vm((messages,) + tile, F32),
                vm((frows, width), F32),
                vm((nw, frows, width), F32),
                vm(tile, F32),
                dma((7,)),
                dma((groups,)),
                dma((groups,)),
                dma((groups,)),
                dma((groups,)),
                dma((messages,)),
                dma((messages,)),
                dma((nw,)),
                dma((nw,)),
            ],
            compiler_params=pltpu.CompilerParams(collective_id=0, has_side_effects=True),
            name="diloco_step",
        )(counts, frag, params[0], first[0], second[0], glob, mom, features[0], cotangent[0])
        return (out[0][None], out[1][None], out[2][None], out[3], out[4])

    held = P("worker", "fsdp", None)
    shared = P("fsdp", None)
    return jax.shard_map(
        step,
        mesh=mesh,
        in_specs=(held, held, held, shared, shared, held, held, P(), P()),
        out_specs=(held, held, held, shared, shared),
        check_vma=False,
    )
```

time: 439 us -> 63.5 us (0.14)
  waiting for transfers between devices: 388 us -> 0 us
  Pallas kernels: 0 us -> 57.8 us
  blocking collectives: 26.4 us -> 0 us
  between operations: 16.1 us -> 1.3 us
    reduce_scatter x1 -> x0, waiting for transfers between devices: 388 us -> none  [body(): summed = lax.psum_scatter(term, 'fsdp', scatter_dimension=0, tiled=True)]
    pallas_call x0 -> x1, Pallas kernels: none -> 57.8 us  [step(): pl.pallas_call(functools.partial(kernel, nw, zs), out_shape=(big, big, bi...]
    psum x1 -> x0, blocking collectives: 26.4 us -> none  [body(): pseudo_grad = lax.psum(drift_term, 'worker') / token_total]
  transfers between devices with their start and end apart: 1 -> 0, of which waited for: 1 -> 0; matrix products, arithmetic and copies ran while one was open for 0% -> 0% of each run, Pallas kernels for 0% -> 0%
where the time goes in v1:
time: 63.5 us; the launch traced here: 63.1 us
  Pallas kernels  57.8 us (91%)
  local copies, waits for them, and re-layouts  4 us (6%)
  between operations  1.3 us (2%)
    pallas_call x1, Pallas kernels, step(): pl.pallas_call(functools.partial(kernel, nw, zs), out_shape=(big, big, bi...  57.8 us
    unnamed x13, local copies, waits for them, and re-layouts  4 us

profile of v1, /device:TPU:8, one launch (start us, length us, event | category | flops | bytes accessed | tf_op | source)
XLA Modules:
  0.0 63.1 jit_solution(1155340970317296056)
XLA Ops:
  1.3 57.8 %diloco_step.1 = (f32[32,128]{1,0:T(8,128)}, f32[32,128]{1,0:T(8,128)}, f32[32,128]{1,0:T(8,128)}, f32[8,128]{1,0:T(8,128)}, f32[8,128]{1,0:T(8,128)}) custom-call(s32[8]{0:T(128)} %counts.1, s32[1]{0:T(128)S(6)} %copy.19.frag_ref, f32[32,128]{1,0:T(8,128)} %bitcast.13, f32[32,128]{1,0:T(8,128)} %bitcast.14, f32[32,128]{1,0:T(8,128)} %bitcast.15, ...), custom_call_target="tpu_custom_call" | custom-call | tf_op jit(solution)/shard_map/diloco_step/pallas_call | solution.py:320
  59.1 0.0 copy-start.1
  59.1 1.3 %copy.20 = f32[1,32,128]{2,1,0:T(8,128)} copy(f32[1,32,128]{2,1,0:T(8,128)} %bitcast.12) | data formatting | bytes 32768
  60.4 0.0 copy-done.1
  60.4 0.0 copy-start
  60.4 0.6 copy.21
  61.0 0.1 copy-done
  61.1 0.0 copy-start.3
  61.1 0.6 copy.22
  61.7 0.1 copy-done.3
  61.8 0.0 copy-start.2
  61.8 0.6 copy.23
  62.4 0.1 copy-done.2
  62.5 0.6 copy.24
Async XLA Ops:
  59.1 1.3 %copy-start.1 = (f32[32,128]{1,0:T(8,128)S(1)}, f32[32,128]{1,0:T(8,128)}, u32[]{:S(2)}) copy-start(f32[32,128]{1,0:T(8,128)} %get-tuple-element.11) | copy-start | bytes 49156
  60.4 0.7 %copy-start = (f32[32,128]{1,0:T(8,128)S(1)}, f32[32,128]{1,0:T(8,128)}, u32[]{:S(2)}) copy-start(f32[32,128]{1,0:T(8,128)} %get-tuple-element.12) | copy-start | bytes 49156
  61.1 0.7 %copy-start.3 = (f32[8,128]{1,0:T(8,128)S(1)}, f32[8,128]{1,0:T(8,128)}, u32[]{:S(2)}) copy-start(f32[8,128]{1,0:T(8,128)} %get-tuple-element.23) | copy-start | bytes 12292
  61.8 0.7 %copy-start.2 = (f32[8,128]{1,0:T(8,128)S(1)}, f32[8,128]{1,0:T(8,128)}, u32[]{:S(2)}) copy-start(f32[8,128]{1,0:T(8,128)} %get-tuple-element.24) | copy-start | bytes 12292

commit v2 on v1

--- a/solution.py
+++ b/solution.py
@@ -22,47 +22,70 @@
 OUTER_RATE = 0.7
 MIXING = 0.5
 
-STRIDE = 3
-GROUP = 4
-
-
-def make_tree(zs, stride):
+VMEM_LIMIT = 16 * 1024 * 1024
+GROUP = 2
+STOPS = {1: (13, 11, 7, 4), -1: (11, 7, 4)}
+
+HOP, WIRE, STOP, FIRST, NEXT = 0.78, 0.35, 0.88, 4.8, 0.71
+
+
+def make_tree(zs):
     steps = {}
     for d, length in ((1, zs // 2), (-1, zs - zs // 2 - 1)):
-        stops = list(range(length, stride - 1, -stride))
-        if not stops:
-            stops = [length]
-        for o in range(length, 0, -1):
+        stops = [0] + [s for s in STOPS[d] if s <= length]
+        for o in range(1, length + 1):
             if o in stops:
-                below = [s for s in stops if s < o]
-                steps[d, o] = o - (max(below) if below else 0)
+                steps[d, o] = o - max(s for s in stops if s < o)
             else:
-                steps[d, o] = 1
+                steps[d, o] = o - min(stops, key=lambda s: (abs(s - o), s))
     return steps
 
 
-def make_order(steps):
+def turn(i, groups):
+    return (groups // 2 + ((i + 1) // 2) * (1 if i % 2 else -1)) % groups
+
+
+def groups_of(d, o, groups):
+    return {((r + d * o) // GROUP) % groups for r in range(GROUP)}
+
+
+def make_order(steps, zs):
+    groups = zs // GROUP
+    arrival = {turn(i, groups): FIRST + NEXT * i for i in range(groups)}
     kids = {}
     for (d, o), s in steps.items():
-        up = (d, o - s) if o - s else (0, 0)
-        kids.setdefault(up, []).append((d, o))
-    half = max(o for _, o in steps)
+        kids.setdefault((d, o - s) if o - s else (0, 0), []).append((d, o))
     ready = {}
-
-    def when(node):
-        if node not in ready:
-            own = 0.3 * (half - node[1])
-            ready[node] = max([own] + [when(k) + 1.0 + 0.8 * steps[k] for k in kids.get(node, [])])
-        return ready[node]
-
-    order = sorted(steps, key=lambda n: (when(n), -n[1], -n[0]))
-    return order, kids
+    left = {n: len(kids.get(n, [])) for n in steps}
+    at = {n: max(arrival[g] for g in groups_of(*n, groups)) for n in steps}
+    events = [(at[n], n, 0) for n in steps if not left[n]]
+    free = {1: 0.0, -1: 0.0}
+    while events:
+        events.sort()
+        t, n, hop = events.pop(0)
+        step = steps[n]
+        if hop == 0:
+            ready[n] = t
+        if hop < abs(step):
+            link = n[0] if step > 0 else -n[0]
+            begin = max(t, free[link])
+            free[link] = begin + WIRE
+            last = hop + 1 == abs(step)
+            events.append((begin + HOP + (WIRE + STOP if last else 0.0), n, hop + 1))
+            continue
+        up = (n[0], n[1] - step)
+        if up[1]:
+            left[up] -= 1
+            at[up] = max(at[up], t)
+            if not left[up]:
+                events.append((at[up], up, 0))
+    return sorted(steps, key=lambda n: (ready[n], -n[1], -n[0])), kids
 
 
 def kernel(
     nw,
     zs,
-    counts,
+    counts_h,
     frag_ref,
     params_h,
     first_h,
@@ -71,11 +94,8 @@
     mom_h,
     feats_h,
     cot_h,
-    new_params,
-    new_first,
-    new_second,
-    new_glob,
-    new_mom,
+    result,
+    counts,
     feats,
     cot,
     params,
@@ -112,8 +132,8 @@
     tokens = feats.shape[0]
     groups = zs // GROUP
 
-    steps = make_tree(zs, STRIDE)
-    order, kids = make_order(steps)
+    steps = make_tree(zs)
+    order, kids = make_order(steps, zs)
     slot = {node: i for i, node in enumerate(steps)}
     lengths = sorted({(d, s) for (d, _), s in steps.items()})
 
@@ -144,12 +164,14 @@
             (first_h, first),
             (second_h, second),
             (mom_h, mom),
+            (counts_h, counts),
         )
     ):
         copy = pltpu.make_async_copy(src, dst, load_sem.at[i])
         copy.start()
         loads.append(copy)
 
+    loads[7].wait()
     live = counts[w]
     live_f = live.astype(F32)
     loads[0].wait()
@@ -158,10 +180,7 @@
     loads[1].wait()
 
     def group_z(i):
-        p = ((i + 1) // 2) * (1 if i % 2 else -1)
-        return ((z // GROUP + groups // 2 + p + groups) % groups) * GROUP
-
-    order_of_groups = [((i + 1) // 2) * (1 if i % 2 else -1) % groups for i in range(groups)]
+        return ((z // GROUP + turn(i, groups)) % groups) * GROUP
 
     def remote(src, dst, send, recv, mate):
         return pltpu.make_async_remote_copy(
@@ -200,17 +219,8 @@
         copy.start()
         x_copies.append(copy)
 
-    multiply(0)
-    pl.semaphore_wait(barrier, len(partners))
-    send_core(0)
-    lag = 3
-    for i in range(1, groups):
+    for i in range(groups):
         multiply(i)
-        send_core(i)
-        if i >= lag:
-            send_x(i - lag)
-    for i in range(max(groups - lag, 0), groups):
-        send_x(i)
 
     loads[2].wait()
     loads[3].wait()
@@ -221,6 +231,12 @@
     mine = live_f * (glob[...] - old)
     drift[...] = mine
     wall[w] = mine
+
+    pl.semaphore_wait(barrier, len(partners))
+    for i in range(groups):
+        send_core(i)
+    for i in range(groups):
+        send_x(i)
     worker_copies = []
     for r in range(1, nw):
         copy = remote(drift, wall.at[w], wsend_sem.at[r], wrecv_sem.at[w], ((w + r) % nw, k))
@@ -240,8 +256,8 @@
         loads[6].wait()
         momentum = NESTEROV * mom[...] + pseudo
         fresh = glob[...] - OUTER_RATE * (pseudo + NESTEROV * momentum)
-        new_mom[...] = momentum
-        new_glob[...] = fresh
+        result[pl.ds(3 * rows + fresh.shape[0], fresh.shape[0]), :] = momentum
+        result[pl.ds(3 * rows, fresh.shape[0]), :] = fresh
         for f in range(FRAGS):
             spread[pl.ds(f, rows // FRAGS, stride=FRAGS), :] = fresh
         loads[4].wait()
@@ -250,10 +266,9 @@
     done = set()
 
     def need(d, o):
-        rel = {((r + d * o) // GROUP) % groups for r in range(GROUP)}
+        where = groups_of(d, o, groups)
         for i in range(groups):
-            where = (groups // 2 + order_of_groups[i]) % groups
-            if where in rel and i not in done:
+            if turn(i, groups) in where and i not in done:
                 done.add(i)
                 x_copies[i].wait_recv()
                 zr = pl.ds(group_z(i), GROUP)
@@ -281,7 +296,7 @@
         copy = remote(src, zrecv.at[i], zsend_sem.at[i], zrecv_sem.at[i], z_mate(d * steps[node]))
         copy.start()
         z_copies[node] = copy
-        if count == (3 * len(order)) // 4:
+        if count == (2 * len(order)) // 3:
             outer()
 
     need(1, 0)
@@ -292,12 +307,25 @@
     before = params[...]
     inner = before - LEARN_RATE * (update + DECAY_RATE * before)
     chosen = lax.broadcasted_iota(jnp.int32, inner.shape, 0) % FRAGS == frag
-    new_params[...] = jnp.where(chosen, MIXING * spread[...] + (1.0 - MIXING) * inner, inner)
-    new_first[...] = first_new
-    new_second[...] = second_new
+    result[pl.ds(0, rows), :] = jnp.where(chosen, MIXING * spread[...] + (1.0 - MIXING) * inner, inner)
+    result[pl.ds(rows, rows), :] = first_new
+    result[pl.ds(2 * rows, rows), :] = second_new
 
     for copy in core_copies + x_copies + worker_copies + list(z_copies.values()):
         copy.wait_send()
+
+
+def hand_out(packed, *refs):
+    outs, sems = refs[:-1], refs[-1]
+    copies, lo = [], 0
+    for i, out in enumerate(outs):
+        n = out.shape[0]
+        copy = pltpu.make_async_copy(packed.at[pl.ds(lo, n)], out, sems.at[i])
+        copy.start()
+        copies.append(copy)
+        lo += n
+    for copy in copies:
+        copy.wait()
 
 
 def solution(mesh):
@@ -313,16 +341,17 @@
         messages = zs - 1
         groups = zs // GROUP
         tile = (rows, width)
+        in_hbm = functools.partial(pltpu.with_memory_space_constraint, memory_space=pltpu.HBM)
         big = jax.ShapeDtypeStruct(tile, F32)
         small = jax.ShapeDtypeStruct((frows, width), F32)
-        smem = pl.BlockSpec(memory_space=pltpu.SMEM)
         hbm = pl.BlockSpec(memory_space=pl.ANY)
-        out = pl.pallas_call(
+        packed = pl.pallas_call(
             functools.partial(kernel, nw, zs),
-            out_shape=(big, big, big, small, small),
-            in_specs=[smem, smem] + [hbm] * 7,
-            out_specs=[pl.BlockSpec(memory_space=vm)] * 5,
+            out_shape=jax.ShapeDtypeStruct((3 * rows + 2 * frows, width), F32),
+            in_specs=[hbm, pl.BlockSpec(memory_space=pltpu.SMEM)] + [hbm] * 7,
+            out_specs=pl.BlockSpec(memory_space=vm),
             scratch_shapes=[
+                pltpu.SMEM((nw,), jnp.int32),
                 vm((tokens, depth), jnp.bfloat16),
                 vm((tokens, width), jnp.bfloat16),
                 vm(tile, F32),
@@ -340,7 +369,7 @@
                 vm((frows, width), F32),
                 vm((nw, frows, width), F32),
                 vm(tile, F32),
-                dma((7,)),
+                dma((8,)),
                 dma((groups,)),
                 dma((groups,)),
                 dma((groups,)),
@@ -350,9 +379,18 @@
                 dma((nw,)),
                 dma((nw,)),
             ],
-            compiler_params=pltpu.CompilerParams(collective_id=0, has_side_effects=True),
+            compiler_params=pltpu.CompilerParams(collective_id=0, has_side_effects=True, vmem_limit_bytes=VMEM_LIMIT),
             name="diloco_step",
-        )(counts, frag, params[0], first[0], second[0], glob, mom, features[0], cotangent[0])
+        )(in_hbm(counts), frag, *map(in_hbm, (params[0], first[0], second[0], glob, mom, features[0], cotangent[0])))
+        out = pl.pallas_call(
+            hand_out,
+            out_shape=(big, big, big, small, small),
+            in_specs=[hbm],
+            out_specs=[hbm] * 5,
+            scratch_shapes=[dma((5,))],
+            compiler_params=pltpu.CompilerParams(vmem_limit_bytes=1024 * 1024),
+            name="hand_out",
+        )(packed)
         return (out[0][None], out[1][None], out[2][None], out[3], out[4])
 
     held = P("worker", "fsdp", None)

time: 63.5 us -> 52.4 us (0.83)
  Pallas kernels: 57.8 us -> 50.9 us
  local copies, waits for them, and re-layouts: 4 us -> 0 us
    pallas_call x1 -> x2, Pallas kernels: 57.8 us -> 50.9 us  [the longest x1 50.2 us: step(): pl.pallas_call(functools.partial(kernel, nw, zs), out_shape=jax.ShapeDtyp...]
    unnamed x13 -> x0, local copies, waits for them, and re-layouts: 4 us -> none
where the time goes in v2:
time: 52.4 us; the launch traced here: 52.2 us
  Pallas kernels  50.9 us (97%)
  between operations  1.29 us (2%)
    pallas_call x1, Pallas kernels, step(): pl.pallas_call(functools.partial(kernel, nw, zs), out_shape=jax.ShapeDtyp...  50.2 us

profile of v2, /device:TPU:8, one launch (start us, length us, event | category | flops | bytes accessed | tf_op | source)
XLA Modules:
  0.0 52.2 jit_solution(8053787371805096542)
XLA Ops:
  1.3 50.2 %diloco_step.1.packed = f32[112,128]{1,0:T(8,128)S(1)} custom-call(s32[8]{0:T(128)} %counts_h.1, s32[1]{0:T(128)S(6)} %copy.14.frag_ref, f32[32,128]{1,0:T(8,128)} %bitcast.10, f32[32,128]{1,0:T(8,128)} %bitcast.11, f32[32,128]{1,0:T(8,128)} %bitcast.12, f32[8,128]{1,0:T(8,128)} %glob_h.1, f32[8,128]{1,0:T(8,128)} %mom_h.1, bf16[128,4096]{1,0:T(8,128)(2,1)} %bitcast.8, ...), custom_call_target="tpu_custom_call" | custom-call | tf_op jit(solution)/shard_map/diloco_step/pallas_call | solution.py:348
  51.5 0.7 %hand_out.1 = (f32[32,128]{1,0:T(8,128)}, f32[32,128]{1,0:T(8,128)}, f32[32,128]{1,0:T(8,128)}, f32[8,128]{1,0:T(8,128)}, f32[8,128]{1,0:T(8,128)}) custom-call(f32[112,128]{1,0:T(8,128)S(1)} %diloco_step.1.packed), custom_call_target="tpu_custom_call" | custom-call | tf_op jit(solution)/shard_map/hand_out/pallas_call | solution.py:385

commit v3 on v2

--- a/solution.py
+++ b/solution.py
@@ -24,9 +24,12 @@
 
 VMEM_LIMIT = 16 * 1024 * 1024
 GROUP = 2
-STOPS = {1: (13, 11, 7, 4), -1: (11, 7, 4)}
-
-HOP, WIRE, STOP, FIRST, NEXT = 0.78, 0.35, 0.88, 4.8, 0.71
+CORE_PARTS = (0, 1, 2, 4, 8, 16)
+X_PARTS = tuple(range(15)) + (16, 18, 20, 22, 24, 28, 32)
+STOPS = {1: (13, 11, 7, 3), -1: (13, 11, 7, 3)}
+NEAR = 2
+
+HOP, WIRE, STOP, FIRST, NEXT, SLACK = 0.78, 0.35, 0.88, 3.9, 0.36, 0.8
 
 
 def make_tree(zs):
@@ -45,19 +48,26 @@
     return (groups // 2 + ((i + 1) // 2) * (1 if i % 2 else -1)) % groups
 
 
+def part_of(bounds, i):
+    return max(p for p, first in enumerate(bounds) if first <= i)
+
+
 def groups_of(d, o, groups):
     return {((r + d * o) // GROUP) % groups for r in range(GROUP)}
 
 
+def far_first(steps):
+    return sorted(list(steps) + [(0, 0)], key=lambda n: (-n[1], -n[0]))
+
+
 def make_order(steps, zs):
-    groups = zs // GROUP
-    arrival = {turn(i, groups): FIRST + NEXT * i for i in range(groups)}
+    arrival = {n: FIRST + NEXT * i for i, n in enumerate(far_first(steps))}
     kids = {}
     for (d, o), s in steps.items():
         kids.setdefault((d, o - s) if o - s else (0, 0), []).append((d, o))
     ready = {}
     left = {n: len(kids.get(n, [])) for n in steps}
-    at = {n: max(arrival[g] for g in groups_of(*n, groups)) for n in steps}
+    at = {n: arrival[n] for n in steps}
     events = [(at[n], n, 0) for n in steps if not left[n]]
     free = {1: 0.0, -1: 0.0}
     while events:
@@ -65,7 +75,7 @@
         t, n, hop = events.pop(0)
         step = steps[n]
         if hop == 0:
-            ready[n] = t
+            ready[n] = t + (SLACK if n in kids else 0.0)
         if hop < abs(step):
             link = n[0] if step > 0 else -n[0]
             begin = max(t, free[link])
@@ -122,6 +132,7 @@
     zrecv_sem,
     wsend_sem,
     wrecv_sem,
+    far_sem,
 ):
     w = lax.axis_index("worker")
     k = lax.axis_index("fsdp")
@@ -134,9 +145,11 @@
 
     steps = make_tree(zs)
     order, kids = make_order(steps, zs)
-    slot = {node: i for i, node in enumerate(steps)}
-    lengths = sorted({(d, s) for (d, _), s in steps.items()})
-
+    slot = {}
+    for kin in kids.values():
+        for node in kin:
+            slot[node] = len(slot)
+    channel = {up: i for i, up in enumerate(kids)}
     def at(x, zz, core):
         return (w, x * (2 * zs) + zz * 2 + core)
 
@@ -146,10 +159,14 @@
     def z_mate(hop):
         return at(xh, (z + hop + zs) % zs, c)
 
-    partners = [core_mate, x_mate]
-    hops = sorted({h for d, s in lengths for h in (d * s, -d * s)})
-    partners += [z_mate(h) for h in hops]
-    partners += [((w + r) % nw, k) for r in range(1, nw)]
+    y, xl, ny = w // 2, w % 2, nw // 2
+    side_mate = (2 * y + 1 - xl, k)
+    up_mate, down_mate = (2 * ((y + 1) % ny) + xl, k), (2 * ((y + ny - 1) % ny) + xl, k)
+    partners = [core_mate, x_mate] + [z_mate(h) for h in (1, -1, NEAR, -NEAR)]
+    if nw > 1:
+        partners.append(side_mate)
+    if ny > 1:
+        partners += [up_mate, down_mate]
     barrier = pltpu.get_barrier_semaphore()
     for mate in partners:
         pl.semaphore_signal(barrier, inc=1, device_id=mate, device_id_type=MESH)
@@ -187,7 +204,7 @@
             src_ref=src, dst_ref=dst, send_sem=send, recv_sem=recv, device_id=mate, device_id_type=MESH
         )
 
-    core_copies, x_copies = [], []
+    core_done, reduced = set(), set()
 
     def multiply(i):
         base = group_z(i)
@@ -207,17 +224,39 @@
 
     def send_core(i):
         zr = pl.ds(group_z(i), GROUP)
-        copy = remote(term.at[1 - c, :, zr], crecv.at[:, zr], csend_sem.at[i], crecv_sem.at[i], core_mate)
+        copy = remote(term.at[1 - c, :, zr], crecv.at[:, zr], csend_sem, crecv_sem.at[part_of(CORE_PARTS, i)], core_mate)
         copy.start()
-        core_copies.append(copy)
+
+    far = far_first(steps)
+
+    def z_of(node):
+        return (z + node[0] * node[1] + zs) % zs
+
+    def reduce_pair(i):
+        part = part_of(CORE_PARTS, i)
+        if part not in core_done:
+            core_done.add(part)
+            wait_core(part)
+        zr = pl.ds(group_z(i), GROUP)
+        chip[:, zr] = term[c, :, zr] + crecv[:, zr]
 
     def send_x(i):
-        zr = pl.ds(group_z(i), GROUP)
-        core_copies[i].wait_recv()
-        chip[:, zr] = term[c, :, zr] + crecv[:, zr]
-        copy = remote(chip.at[1 - xh, zr], xrecv.at[zr], xsend_sem.at[i], xrecv_sem.at[i], x_mate)
-        copy.start()
-        x_copies.append(copy)
+        where = groups_of(*far[i], groups)
+        for j in range(groups):
+            if turn(j, groups) in where and j not in reduced:
+                reduced.add(j)
+                reduce_pair(j)
+        zz = z_of(far[i])
+        remote(chip.at[1 - xh, zz], xrecv.at[zz], xsend_sem, xrecv_sem.at[part_of(X_PARTS, i)], x_mate).start()
+
+    def wait_core(part):
+        n = GROUP * (CORE_PARTS[part + 1] - CORE_PARTS[part])
+        zr = pl.ds(0, n)
+        remote(term.at[1 - c, :, zr], crecv.at[:, zr], csend_sem, crecv_sem.at[part], core_mate).wait_recv()
+
+    def wait_x(part):
+        zr = pl.ds(0, X_PARTS[part + 1] - X_PARTS[part])
+        remote(chip.at[1 - xh, zr], xrecv.at[zr], xsend_sem, xrecv_sem.at[part], x_mate).wait_recv()
 
     for i in range(groups):
         multiply(i)
@@ -235,18 +274,32 @@
     pl.semaphore_wait(barrier, len(partners))
     for i in range(groups):
         send_core(i)
-    for i in range(groups):
+    for h in (NEAR, -NEAR):
+        pl.semaphore_signal(far_sem, inc=1, device_id=z_mate(h), device_id_type=MESH)
+    if nw > 1:
+        remote(drift, wall.at[w], wsend_sem.at[0], wrecv_sem.at[0], side_mate).start()
+    for i in range(zs):
         send_x(i)
-    worker_copies = []
-    for r in range(1, nw):
-        copy = remote(drift, wall.at[w], wsend_sem.at[r], wrecv_sem.at[w], ((w + r) % nw, k))
-        copy.start()
-        worker_copies.append(copy)
+
+    def block(i):
+        return wall.at[pl.ds(2 * ((y + i + ny) % ny), 2)]
+
+    def worker_pairs():
+        if nw > 1:
+            remote(drift, drift, wsend_sem.at[0], wrecv_sem.at[0], side_mate).wait_recv()
+        if ny > 1:
+            remote(block(0), block(0), wsend_sem.at[1], wrecv_sem.at[1], up_mate).start()
+            remote(block(0), block(0), wsend_sem.at[2], wrecv_sem.at[2], down_mate).start()
+
+    def worker_relay():
+        if ny > 1:
+            remote(block(-1), block(-1), wsend_sem.at[0], wrecv_sem.at[1], up_mate).wait_recv()
+            remote(block(-1), block(-1), wsend_sem.at[3], wrecv_sem.at[3], up_mate).start()
 
     def outer():
-        for r in range(1, nw):
-            sender = (w + r) % nw
-            remote(drift, wall.at[sender], wsend_sem.at[r], wrecv_sem.at[sender], (sender, k)).wait_recv()
+        if ny > 1:
+            remote(block(1), block(1), wsend_sem.at[0], wrecv_sem.at[2], down_mate).wait_recv()
+            remote(block(2), block(2), wsend_sem.at[0], wrecv_sem.at[3], up_mate).wait_recv()
         total = wall[0]
         token_total = counts[0]
         for i in range(1, nw):
@@ -265,41 +318,46 @@
 
     done = set()
 
-    def need(d, o):
-        where = groups_of(d, o, groups)
-        for i in range(groups):
-            if turn(i, groups) in where and i not in done:
-                done.add(i)
-                x_copies[i].wait_recv()
-                zr = pl.ds(group_z(i), GROUP)
-                own[zr] = chip[xh, zr] + xrecv[zr]
-
-    z_copies = {}
+    def need(node):
+        part = part_of(X_PARTS, far.index(node))
+        if part not in done:
+            done.add(part)
+            wait_x(part)
+            for other in far[X_PARTS[part] : X_PARTS[part + 1]]:
+                zz = z_of(other)
+                own[zz] = chip[xh, zz] + xrecv[zz]
 
     def gather(node, zz):
+        kin = kids[node]
+        lo = slot[kin[0]]
+        zr = pl.ds(lo, len(kin))
+        remote(zrecv.at[zr], zrecv.at[zr], zsend_sem, zrecv_sem.at[channel[node]], x_mate).wait_recv()
         total = own[zz]
-        for kid in kids.get(node, []):
-            z_copies[kid].wait_recv()
-            total = total + zrecv[slot[kid]]
+        for i in range(lo, lo + len(kin)):
+            total = total + zrecv[i]
         return total
 
+    pl.semaphore_wait(far_sem, 2)
     for count, node in enumerate(order):
         d, o = node
-        need(d, o)
-        zz = (z + d * o + zs) % zs
+        need(node)
+        zz = z_of(node)
         i = slot[node]
         if kids.get(node):
             zsend[i] = gather(node, zz)
             src = zsend.at[i]
         else:
             src = own.at[zz]
-        copy = remote(src, zrecv.at[i], zsend_sem.at[i], zrecv_sem.at[i], z_mate(d * steps[node]))
-        copy.start()
-        z_copies[node] = copy
-        if count == (2 * len(order)) // 3:
+        up = (d, o - steps[node]) if o - steps[node] else (0, 0)
+        remote(src, zrecv.at[i], zsend_sem, zrecv_sem.at[channel[up]], z_mate(d * steps[node])).start()
+        if count == len(order) // 3:
+            worker_pairs()
+        if count == len(order) // 2:
+            worker_relay()
+        if count == (3 * len(order)) // 4:
             outer()
 
-    need(1, 0)
+    need((0, 0))
     gradient = gather((0, 0), z) / live_f
     first_new = BETA_ONE * first[...] + (1.0 - BETA_ONE) * gradient
     second_new = BETA_TWO * second[...] + (1.0 - BETA_TWO) * gradient * gradient
@@ -311,8 +369,13 @@
     result[pl.ds(rows, rows), :] = first_new
     result[pl.ds(2 * rows, rows), :] = second_new
 
-    for copy in core_copies + x_copies + worker_copies + list(z_copies.values()):
-        copy.wait_send()
+    remote(crecv, crecv, csend_sem, crecv_sem.at[0], core_mate).wait_send()
+    remote(xrecv, xrecv, xsend_sem, xrecv_sem.at[0], x_mate).wait_send()
+    remote(zrecv, zrecv, zsend_sem, zrecv_sem.at[0], x_mate).wait_send()
+    if nw > 1:
+        remote(drift, drift, wsend_sem.at[0], wrecv_sem.at[0], side_mate).wait_send()
+    for i in range(1, 4 if ny > 1 else 0):
+        remote(block(0), block(0), wsend_sem.at[i], wrecv_sem.at[i], up_mate).wait_send()
 
 
 def hand_out(packed, *refs):
@@ -339,6 +402,7 @@
         vm = pltpu.VMEM
         dma = pltpu.SemaphoreType.DMA
         messages = zs - 1
+        stops = len(make_order(make_tree(zs), zs)[1])
         groups = zs // GROUP
         tile = (rows, width)
         in_hbm = functools.partial(pltpu.with_memory_space_constraint, memory_space=pltpu.HBM)
@@ -370,14 +434,15 @@
                 vm((nw, frows, width), F32),
                 vm(tile, F32),
                 dma((8,)),
-                dma((groups,)),
-                dma((groups,)),
-                dma((groups,)),
-                dma((groups,)),
-                dma((messages,)),
-                dma((messages,)),
-                dma((nw,)),
-                dma((nw,)),
+                dma(()),
+                dma((len(CORE_PARTS) - 1,)),
+                dma(()),
+                dma((len(X_PARTS) - 1,)),
+                dma(()),
+                dma((stops,)),
+                dma((4,)),
+                dma((4,)),
+                pltpu.SemaphoreType.REGULAR,
             ],
             compiler_params=pltpu.CompilerParams(collective_id=0, has_side_effects=True, vmem_limit_bytes=VMEM_LIMIT),
             name="diloco_step",

time: 52.4 us -> 50.5 us (0.964)
  the two profiles are of different devices: /device:TPU:8 before, /device:TPU:2 now
where the time goes in v3:
time: 50.5 us; the launch traced here: 50.4 us
  Pallas kernels  49.1 us (97%)
  between operations  1.29 us (3%)
    pallas_call x1, Pallas kernels, step(): pl.pallas_call(functools.partial(kernel, nw, zs), out_shape=jax.ShapeDtyp...  48.4 us

profile of v3, /device:TPU:2, one launch (start us, length us, event | category | flops | bytes accessed | tf_op | source)
XLA Modules:
  0.0 50.4 jit_solution(2762569812932895189)
XLA Ops:
  1.3 48.4 %diloco_step.1.packed = f32[112,128]{1,0:T(8,128)S(1)} custom-call(s32[8]{0:T(128)} %counts_h.1, s32[1]{0:T(128)S(6)} %copy.14.frag_ref, f32[32,128]{1,0:T(8,128)} %bitcast.10, f32[32,128]{1,0:T(8,128)} %bitcast.11, f32[32,128]{1,0:T(8,128)} %bitcast.12, f32[8,128]{1,0:T(8,128)} %glob_h.1, f32[8,128]{1,0:T(8,128)} %mom_h.1, bf16[128,4096]{1,0:T(8,128)(2,1)} %bitcast.8, ...), custom_call_target="tpu_custom_call" | custom-call | tf_op jit(solution)/shard_map/diloco_step/pallas_call | solution.py:412
  49.7 0.7 %hand_out.1 = (f32[32,128]{1,0:T(8,128)}, f32[32,128]{1,0:T(8,128)}, f32[32,128]{1,0:T(8,128)}, f32[8,128]{1,0:T(8,128)}, f32[8,128]{1,0:T(8,128)}) custom-call(f32[112,128]{1,0:T(8,128)S(1)} %diloco_step.1.packed), custom_call_target="tpu_custom_call" | custom-call | tf_op jit(solution)/shard_map/hand_out/pallas_call | solution.py:450

commit v4 on v3

--- a/solution.py
+++ b/solution.py
@@ -25,11 +25,11 @@
 VMEM_LIMIT = 16 * 1024 * 1024
 GROUP = 2
 CORE_PARTS = (0, 1, 2, 4, 8, 16)
-X_PARTS = tuple(range(15)) + (16, 18, 20, 22, 24, 28, 32)
-STOPS = {1: (13, 11, 7, 3), -1: (13, 11, 7, 3)}
+X_PARTS = tuple(range(9)) + (10, 12, 14, 16, 18, 20, 24, 28, 32)
+STOPS = {1: (12, 8, 4), -1: (12, 8, 4)}
 NEAR = 2
 
-HOP, WIRE, STOP, FIRST, NEXT, SLACK = 0.78, 0.35, 0.88, 3.9, 0.36, 0.8
+HOP, WIRE, STOP, FIRST, NEXT, SLACK = 0.78, 0.35, 0.88, 5.0, 0.36, -1.5
 
 
 def make_tree(zs):
@@ -146,10 +146,16 @@
     steps = make_tree(zs)
     order, kids = make_order(steps, zs)
     slot = {}
-    for kin in kids.values():
-        for node in kin:
+    leaves, trunk = {}, {}
+    for up, kin in kids.items():
+        leaves[up] = [n for n in kin if n not in kids]
+        trunk[up] = [n for n in kin if n in kids]
+        for node in leaves[up] + trunk[up]:
             slot[node] = len(slot)
     channel = {up: i for i, up in enumerate(kids)}
+    for kin in trunk.values():
+        for node in kin:
+            channel[node, 0], channel[node, 1] = len(channel), len(channel) + 1
     def at(x, zz, core):
         return (w, x * (2 * zs) + zz * 2 + core)
 
@@ -176,19 +182,19 @@
         (
             (cot_h, cot),
             (feats_h, feats),
+            (counts_h, counts),
             (params_h, params),
             (glob_h, glob),
             (first_h, first),
             (second_h, second),
             (mom_h, mom),
-            (counts_h, counts),
         )
     ):
-        copy = pltpu.make_async_copy(src, dst, load_sem.at[i])
+        copy = pltpu.make_async_copy(src, dst, load_sem.at[min(i, 3)])
         copy.start()
         loads.append(copy)
 
-    loads[7].wait()
+    loads[2].wait()
     live = counts[w]
     live_f = live.astype(F32)
     loads[0].wait()
@@ -261,8 +267,7 @@
     for i in range(groups):
         multiply(i)
 
-    loads[2].wait()
-    loads[3].wait()
+    pltpu.make_async_copy(result, result, load_sem.at[3]).wait()
     frag = frag_ref[0]
     old = params[pl.ds(0, rows // FRAGS, stride=FRAGS), :]
     for f in range(1, FRAGS):
@@ -306,15 +311,12 @@
             total = total + wall[i]
             token_total = token_total + counts[i]
         pseudo = total / token_total.astype(F32)
-        loads[6].wait()
         momentum = NESTEROV * mom[...] + pseudo
         fresh = glob[...] - OUTER_RATE * (pseudo + NESTEROV * momentum)
         result[pl.ds(3 * rows + fresh.shape[0], fresh.shape[0]), :] = momentum
         result[pl.ds(3 * rows, fresh.shape[0]), :] = fresh
         for f in range(FRAGS):
             spread[pl.ds(f, rows // FRAGS, stride=FRAGS), :] = fresh
-        loads[4].wait()
-        loads[5].wait()
 
     done = set()
 
@@ -328,37 +330,43 @@
                 own[zz] = chip[xh, zz] + xrecv[zz]
 
     def gather(node, zz):
-        kin = kids[node]
-        lo = slot[kin[0]]
-        zr = pl.ds(lo, len(kin))
+        kin = leaves[node]
+        zr = pl.ds(slot[kin[0]], len(kin))
         remote(zrecv.at[zr], zrecv.at[zr], zsend_sem, zrecv_sem.at[channel[node]], x_mate).wait_recv()
         total = own[zz]
-        for i in range(lo, lo + len(kin)):
-            total = total + zrecv[i]
-        return total
-
+        for kid in kin:
+            total = total + zrecv[slot[kid]]
+        for half in range(2):
+            hr = pl.ds(half * (rows // 2), rows // 2)
+            part = total[half * (rows // 2) : (half + 1) * (rows // 2)]
+            for kid in trunk[node]:
+                piece = zrecv.at[slot[kid], hr]
+                remote(piece, piece, zsend_sem, zrecv_sem.at[channel[kid, half]], x_mate).wait_recv()
+                part = part + zrecv[slot[kid], hr]
+            yield hr, half, part
+
+    worker_pairs()
     pl.semaphore_wait(far_sem, 2)
     for count, node in enumerate(order):
         d, o = node
         need(node)
         zz = z_of(node)
         i = slot[node]
-        if kids.get(node):
-            zsend[i] = gather(node, zz)
-            src = zsend.at[i]
+        up = (d, o - steps[node]) if o - steps[node] else (0, 0)
+        mate = z_mate(d * steps[node])
+        if node in kids:
+            for hr, half, part in gather(node, zz):
+                zsend[i, hr] = part
+                sem = zrecv_sem.at[channel[node, half]]
+                remote(zsend.at[i, hr], zrecv.at[i, hr], zsend_sem, sem, mate).start()
         else:
-            src = own.at[zz]
-        up = (d, o - steps[node]) if o - steps[node] else (0, 0)
-        remote(src, zrecv.at[i], zsend_sem, zrecv_sem.at[channel[up]], z_mate(d * steps[node])).start()
-        if count == len(order) // 3:
-            worker_pairs()
-        if count == len(order) // 2:
+            remote(own.at[zz], zrecv.at[i], zsend_sem, zrecv_sem.at[channel[up]], mate).start()
+        if count == 4:
             worker_relay()
-        if count == (3 * len(order)) // 4:
-            outer()
 
     need((0, 0))
-    gradient = gather((0, 0), z) / live_f
+    outer()
+    gradient = jnp.concatenate([part for _, _, part in gather((0, 0), z)]) / live_f
     first_new = BETA_ONE * first[...] + (1.0 - BETA_ONE) * gradient
     second_new = BETA_TWO * second[...] + (1.0 - BETA_TWO) * gradient * gradient
     update = first_new / CORRECT_ONE / (jnp.sqrt(second_new / CORRECT_TWO) + ADAM_EPS)
@@ -402,7 +410,7 @@
         vm = pltpu.VMEM
         dma = pltpu.SemaphoreType.DMA
         messages = zs - 1
-        stops = len(make_order(make_tree(zs), zs)[1])
+        stops = 3 * len(make_order(make_tree(zs), zs)[1])
         groups = zs // GROUP
         tile = (rows, width)
         in_hbm = functools.partial(pltpu.with_memory_space_constraint, memory_space=pltpu.HBM)
@@ -433,7 +441,7 @@
                 vm((frows, width), F32),
                 vm((nw, frows, width), F32),
                 vm(tile, F32),
-                dma((8,)),
+                dma((4,)),
                 dma(()),
                 dma((len(CORE_PARTS) - 1,)),
                 dma(()),

time: 50.5 us -> 49 us (0.970)
  Pallas kernels: 49.1 us -> 47.6 us
    pallas_call x1, Pallas kernels: 48.4 us -> 46.9 us  [step(): pl.pallas_call(functools.partial(kernel, nw, zs), out_shape=jax.ShapeDtyp...]
where the time goes in v4:
time: 49 us; the launch traced here: 48.9 us
  Pallas kernels  47.6 us (97%)
  between operations  1.29 us (3%)
    pallas_call x1, Pallas kernels, step(): pl.pallas_call(functools.partial(kernel, nw, zs), out_shape=jax.ShapeDtyp...  46.9 us

profile of v4, /device:TPU:2, one launch (start us, length us, event | category | flops | bytes accessed | tf_op | source)
XLA Modules:
  0.0 48.9 jit_solution(17732932080825485842)
XLA Ops:
  1.3 46.9 %diloco_step.1.packed = f32[112,128]{1,0:T(8,128)S(1)} custom-call(s32[8]{0:T(128)} %counts_h.1, s32[1]{0:T(128)S(6)} %copy.14.frag_ref, f32[32,128]{1,0:T(8,128)} %bitcast.10, f32[32,128]{1,0:T(8,128)} %bitcast.11, f32[32,128]{1,0:T(8,128)} %bitcast.12, f32[8,128]{1,0:T(8,128)} %glob_h.1, f32[8,128]{1,0:T(8,128)} %mom_h.1, bf16[128,4096]{1,0:T(8,128)(2,1)} %bitcast.8, ...), custom_call_target="tpu_custom_call" | custom-call | tf_op jit(solution)/shard_map/diloco_step/pallas_call | solution.py:420
  48.2 0.7 %hand_out.1 = (f32[32,128]{1,0:T(8,128)}, f32[32,128]{1,0:T(8,128)}, f32[32,128]{1,0:T(8,128)}, f32[8,128]{1,0:T(8,128)}, f32[8,128]{1,0:T(8,128)}) custom-call(f32[112,128]{1,0:T(8,128)S(1)} %diloco_step.1.packed), custom_call_target="tpu_custom_call" | custom-call | tf_op jit(solution)/shard_map/hand_out/pallas_call | solution.py:458

commit v5 on v4

--- a/solution.py
+++ b/solution.py
@@ -29,7 +29,7 @@
 STOPS = {1: (12, 8, 4), -1: (12, 8, 4)}
 NEAR = 2
 
-HOP, WIRE, STOP, FIRST, NEXT, SLACK = 0.78, 0.35, 0.88, 5.0, 0.36, -1.5
+HOP, WIRE, STOP, FIRST, NEXT, SLACK = 0.78, 0.35, 0.88, 5.0, 0.36, -0.7
 
 
 def make_tree(zs):

time: 49 us -> 48.7 us (level)
  the two profiles are of different devices: /device:TPU:2 before, /device:TPU:8 now
where the time goes in v5:
time: 48.7 us; the launch traced here: 48.5 us
  Pallas kernels  47.2 us (97%)
  between operations  1.29 us (3%)
    pallas_call x1, Pallas kernels, step(): pl.pallas_call(functools.partial(kernel, nw, zs), out_shape=jax.ShapeDtyp...  46.5 us

profile of v5, /device:TPU:8, one launch (start us, length us, event | category | flops | bytes accessed | tf_op | source)
XLA Modules:
  0.0 48.5 jit_solution(13331265968027328014)
XLA Ops:
  1.3 46.5 %diloco_step.1.packed = f32[112,128]{1,0:T(8,128)S(1)} custom-call(s32[8]{0:T(128)} %counts_h.1, s32[1]{0:T(128)S(6)} %copy.14.frag_ref, f32[32,128]{1,0:T(8,128)} %bitcast.10, f32[32,128]{1,0:T(8,128)} %bitcast.11, f32[32,128]{1,0:T(8,128)} %bitcast.12, f32[8,128]{1,0:T(8,128)} %glob_h.1, f32[8,128]{1,0:T(8,128)} %mom_h.1, bf16[128,4096]{1,0:T(8,128)(2,1)} %bitcast.8, ...), custom_call_target="tpu_custom_call" | custom-call | tf_op jit(solution)/shard_map/diloco_step/pallas_call | solution.py:420
  47.8 0.7 %hand_out.1 = (f32[32,128]{1,0:T(8,128)}, f32[32,128]{1,0:T(8,128)}, f32[32,128]{1,0:T(8,128)}, f32[8,128]{1,0:T(8,128)}, f32[8,128]{1,0:T(8,128)}) custom-call(f32[112,128]{1,0:T(8,128)S(1)} %diloco_step.1.packed), custom_call_target="tpu_custom_call" | custom-call | tf_op jit(solution)/shard_map/hand_out/pallas_call | solution.py:458

commit v6 on v5

--- a/solution.py
+++ b/solution.py
@@ -26,7 +26,7 @@
 GROUP = 2
 CORE_PARTS = (0, 1, 2, 4, 8, 16)
 X_PARTS = tuple(range(9)) + (10, 12, 14, 16, 18, 20, 24, 28, 32)
-STOPS = {1: (12, 8, 4), -1: (12, 8, 4)}
+STOPS = {1: (12, 8, 4), -1: (11, 7, 4)}
 NEAR = 2
 
 HOP, WIRE, STOP, FIRST, NEXT, SLACK = 0.78, 0.35, 0.88, 5.0, 0.36, -0.7

time: 48.7 us -> 48.7 us (level)
  no operation moved by 1% of the time
where the time goes in v6:
time: 48.7 us; the launch traced here: 48.5 us
  Pallas kernels  47.3 us (97%)
  between operations  1.29 us (3%)
    pallas_call x1, Pallas kernels, step(): pl.pallas_call(functools.partial(kernel, nw, zs), out_shape=jax.ShapeDtyp...  46.6 us

profile of v6, /device:TPU:8, one launch (start us, length us, event | category | flops | bytes accessed | tf_op | source)
XLA Modules:
  0.0 48.5 jit_solution(5138301194159739258)
XLA Ops:
  1.3 46.6 %diloco_step.1.packed = f32[112,128]{1,0:T(8,128)S(1)} custom-call(s32[8]{0:T(128)} %counts_h.1, s32[1]{0:T(128)S(6)} %copy.14.frag_ref, f32[32,128]{1,0:T(8,128)} %bitcast.10, f32[32,128]{1,0:T(8,128)} %bitcast.11, f32[32,128]{1,0:T(8,128)} %bitcast.12, f32[8,128]{1,0:T(8,128)} %glob_h.1, f32[8,128]{1,0:T(8,128)} %mom_h.1, bf16[128,4096]{1,0:T(8,128)(2,1)} %bitcast.8, ...), custom_call_target="tpu_custom_call" | custom-call | tf_op jit(solution)/shard_map/diloco_step/pallas_call | solution.py:420
  47.9 0.7 %hand_out.1 = (f32[32,128]{1,0:T(8,128)}, f32[32,128]{1,0:T(8,128)}, f32[32,128]{1,0:T(8,128)}, f32[8,128]{1,0:T(8,128)}, f32[8,128]{1,0:T(8,128)}) custom-call(f32[112,128]{1,0:T(8,128)S(1)} %diloco_step.1.packed), custom_call_target="tpu_custom_call" | custom-call | tf_op jit(solution)/shard_map/hand_out/pallas_call | solution.py:458
